TPU v7x, 128 devices: a whole 4x4x4 slice. The times are simulated.
128 devices in a mesh: row: 8 (over x, z_hi), col: 16 (over z_lo, y, core).
Axes of the slice: x: 4, y: 4, z: 4 (z_hi: 2, z_lo: 2; z = z_hi * 2 + z_lo), core: 2. Of those that a mesh axis runs over, the one named last changes fastest.
Arguments:
- contact_map: bfloat16 [1024, 1024, 128], P('row', 'col'), may hold values from -6 to 6
- kernel_near: bfloat16 [3, 3, 128, 128], replicated, may hold values from -0.25 to 0.25
- offset_near: float32 [128], replicated, may hold values from -3 to 3
- kernel_mid: bfloat16 [3, 3, 128, 128], replicated, may hold values from -0.25 to 0.25
- offset_mid: float32 [128], replicated, may hold values from -3 to 3
- kernel_far: bfloat16 [3, 3, 128, 128], replicated, may hold values from -0.25 to 0.25
- offset_far: float32 [128], replicated, may hold values from -3 to 3
Outputs:
- refined: bfloat16 [1024, 1024, 128], P('row', 'col')
All inputs are finite; a program needn't handle non-finite values.
Results may differ from a plain program's by a relative error of at most 0.013.
Values may be sent and summed in bfloat16 or wider, within the bound.
A program may use at most 64 MiB of HBM per device.

v0:
```python
import jax
import jax.numpy as jnp
from jax import lax
from jax.experimental import pallas as pl
from jax.experimental.pallas import tpu as pltpu
from jax.sharding import PartitionSpec as P

MESH = pl.DeviceIdType.MESH
F32, BF16 = jnp.float32, jnp.bfloat16

FLIPS = {
    "x0": ((1, 0, 0), 2),
    "x1": ((3, 0, 0), 6),
    "y0": ((0, 1, 0), 1),
    "y1": ((0, 3, 0), 3),
    "z0": ((0, 0, 1), 4),
    "z1": ((0, 0, 3), 5),
}
PATHS = {
    1: ("y0z1 z0", "z0z1 y0"),
    2: ("y1 x0y0", "y0y1 x0"),
    3: ("x0z1 y1z0", "z0z1 x0y1"),
    4: ("x1z0 x0", "x0x1z0"),
    5: ("x1z1 y0 x0", "x0y0z1 x1"),
    6: ("y1 y0z0 x1", "z0 x1y0y1"),
    7: ("x1y1z1", "y1z1 x1"),
}
STEPS = 8
ROWS = 16
LAG = (2, 2, 4)
SLOTS = len(LAG)


def segment(text):
    flips, change = [0, 0, 0], 0
    for at in range(0, len(text), 2):
        move, turn = FLIPS[text[at : at + 2]]
        flips = [a ^ b for a, b in zip(flips, move)]
        change ^= turn
    return tuple(flips), change


def plan():
    hops = []
    for start, paths in PATHS.items():
        for path, text in enumerate(paths):
            here, came = start, None
            for depth, part in enumerate(text.split()):
                flips, change = segment(part)
                hops.append([start, path, depth, here, flips, came])
                here, came = here ^ change, flips
            hops.append([start, path, depth + 1, here, None, came])
    relays = {w: [] for w in range(8)}
    for start, path, depth, here, flips, came in hops:
        if depth and flips is not None:
            relays[here].append((depth, start, path))
    slot = {}
    for w, held in relays.items():
        held.sort()
        taken = set()
        for depth, start, path in held:
            options = (2,) if depth == 2 else (0, 1, 2)
            at = [s for s in options if s not in taken][0]
            taken.add(at)
            slot[start, path, depth] = at
    out = [[0] * 8 for _ in range(2 + SLOTS)]
    into = [[0] * 8 for _ in range(2 + SLOTS)]
    code = lambda f: f[0] + 4 * f[1] + 16 * f[2]
    for start, path, depth, here, flips, came in hops:
        own = path if depth == 0 else None if flips is None else 2 + slot[start, path, depth]
        if flips is not None:
            after = slot.get((start, path, depth + 1))
            final = after is None
            out[own][here] = code(flips) + 64 * final + 128 * (path if final else after) + 512
        if came is not None:
            into[path if flips is None else own][here] = code(came) + 512
    return out, into


OUT, INTO = plan()


def pick(w, values):
    result = jnp.int32(values[0])
    for k in range(1, 8):
        result = jnp.where(w == k, jnp.int32(values[k]), result)
    return result


def both(a, b):
    return jnp.logical_and(a, b)


def flipped(value, by):
    return ((value // 2 + by // 2) % 2) * 2 + (value + by) % 2


ALL, LEFT, RIGHT = slice(0, 64), slice(0, 8), slice(56, 64)
HALO = []
for lo, hi in ((0, 32), (32, 128)):
    HALO.append((0, -1, slice(lo, hi), LEFT, "r", slice(8 + lo, 8 + hi)))
    HALO.append((0, 1, slice(lo, hi), RIGHT, "l", slice(8 + lo, 8 + hi)))
for di, src, dst in ((1, slice(120, 128), slice(0, 8)), (-1, slice(0, 8), slice(136, 144))):
    HALO.append((di, 0, src, ALL, "c", dst))
    HALO.append((di, -1, src, LEFT, "r", dst))
    HALO.append((di, 1, src, RIGHT, "l", dst))


def kernel(
    x, k1, b1, k2, b2, k3, b3, out,
    xc, xl, xr, x3, l1, l2, direct, turned, inside, w1, w2, w3, bufs, result,
    load_sem, halo_send, halo_recv, send_sem, recv_sem, out_sem,
):
    i, j = lax.axis_index("row"), lax.axis_index("col")
    cx, cy, cz, core = i // 2, (j // 2) % 4, (i % 2) * 2 + j // 8, j % 2
    u1 = (cx // 2 + cz) % 2
    u2 = (cx + cy // 2) % 2
    u3 = (cy + cz // 2) % 2
    w = u1 * 4 + u2 * 2 + u3
    fixed = w == 0

    def chip(flips, c):
        x_ = flipped(cx, flips % 4)
        y_ = flipped(cy, (flips // 4) % 4)
        z_ = flipped(cz, (flips // 16) % 4)
        return (x_ * 2 + z_ // 2, (z_ % 2) * 8 + y_ * 2 + c)

    loads = [(x, xc.at[8:136])]
    for k, wide in ((k1, w1), (k2, w2)):
        loads.append((k, wide.at[0:1152, 0:128]))
        loads.append((k, wide.at[384:1536, 128:256]))
    loads.append((k3, w3.at[:, 0:128]))
    for a in range(3):
        for e in range(3):
            loads.append(
                (k3.at[pl.ds((e * 3 + a) * 128, 128)], w3.at[pl.ds((a * 3 + e) * 128, 128), 128:256])
            )
    loads = [pltpu.make_async_copy(s, d, load_sem.at[n]) for n, (s, d) in enumerate(loads)]
    for copy in loads:
        copy.start()

    barrier = pltpu.get_barrier_semaphore()
    out_codes = [pick(w, v) for v in OUT]
    in_codes = [pick(w, v) for v in INTO]

    def greet(device):
        pl.semaphore_signal(barrier, 1, device_id=device, device_id_type=MESH)

    def exists(di, dj):
        ok = None
        for ok_ in ([i + di >= 0, i + di < 8] if di else []) + ([j + dj >= 0, j + dj < 16] if dj else []):
            ok = ok_ if ok is None else both(ok, ok_)
        return ok

    expected = jnp.int32(0)
    for di in (-1, 0, 1):
        for dj in (-1, 0, 1):
            if di or dj:
                ok = exists(di, dj)
                expected = expected + jnp.where(ok, 1, 0)
                pl.when(ok)(lambda di=di, dj=dj: greet((i + di, j + dj)))

    @pl.when(fixed)
    def _():
        greet((i, j + 1 - 2 * core))

    expected = expected + jnp.where(fixed, 1, 0)
    for n in range(2 + SLOTS):
        came, goes = in_codes[n], out_codes[n]

        @pl.when(came >= 512)
        def _():
            if n < 2:
                greet(chip(came, 0))
                greet(chip(came, 1))
            else:
                greet(chip(came, core))

        expected = expected + jnp.where(goes >= 512, 1 + (goes // 64) % 2, 0)
    pl.semaphore_wait(barrier, expected)

    targets = {"c": xc, "l": xl, "r": xr}
    halo = []
    for n, (di, dj, rows, cols, name, into) in enumerate(HALO):
        copy = pltpu.make_async_remote_copy(
            x.at[rows, cols],
            targets[name].at[into],
            halo_send.at[n],
            halo_recv.at[n],
            device_id=(i + di, j + dj),
            device_id_type=MESH,
        )
        goes, comes = exists(di, dj), exists(-di, -dj)
        halo.append((copy, goes, comes))
        pl.when(goes)(copy.start)

        @pl.when(jnp.logical_not(comes))
        def _():
            ref = targets[name].at[into]
            ref[...] = jnp.zeros(ref.shape, BF16)

    for wide in (w1, w2):
        wide[1152:1536, 0:128] = jnp.zeros((384, 128), BF16)
        wide[0:384, 128:256] = jnp.zeros((384, 128), BF16)
    column = lax.broadcasted_iota(jnp.int32, (80, 128), 0) + (j * 64 - 8)
    inside[...] = jnp.where(both(column >= 0, column < 1024), 1.0, 0.0).astype(F32)
    for copy in loads:
        copy.wait()

    def halo_wait(ns):
        for n in ns:
            copy, _, comes = halo[n]
            pl.when(comes)(copy.wait_recv)

    def spread(row):
        v = jnp.concatenate([xl[row].astype(F32), xc[row].astype(F32), xr[row].astype(F32)], axis=0)
        x3[row, :, 0:128] = pltpu.roll(v, 1, 0).astype(BF16)
        x3[row, :, 128:256] = v.astype(BF16)
        x3[row, :, 256:384] = pltpu.roll(v, 79, 0).astype(BF16)

    def pair_conv(ref, wide, bias, rows, d):
        lhs = jnp.concatenate(
            [jnp.concatenate([ref[r + (n - 1) * d] for n in range(4)], axis=-1) for r in rows], axis=0
        )
        total = jnp.dot(lhs, wide[...], preferred_element_type=F32)
        keep = inside[...]
        done = []
        for n, r in enumerate(rows):
            for m in range(2):
                v = total[n * 80 : n * 80 + 80, m * 128 : m * 128 + 128]
                done.append((r + m * d, jnp.maximum(v + bias[...], 0.0) * keep))
        return done

    def near(base, count):
        for row, v in pair_conv(x3, w1, b1, [base + 2 * n for n in range(count // 2)], 1):
            l1[row, :, 0:128] = pltpu.roll(v, 2, 0).astype(BF16)
            l1[row, :, 128:256] = v.astype(BF16)
            l1[row, :, 256:384] = pltpu.roll(v, 78, 0).astype(BF16)

    def middle(base, count):
        rows = [base + 4 * n + s for n in range(count // 4) for s in range(2)]
        for row, v in pair_conv(l1, w2, b2, rows, 2):
            l2[row, :, 0:128] = pltpu.roll(v, 4, 0)[8:72].astype(BF16)
            l2[row, :, 128:256] = v[8:72].astype(BF16)
            l2[row, :, 256:384] = pltpu.roll(v, 76, 0)[8:72].astype(BF16)

    def far(t):
        base = t * ROWS
        lhs = jnp.concatenate(
            [jnp.concatenate([l2[base + 8 + r + 4 * a] for a in (-1, 0, 1)], axis=-1) for r in range(ROWS)], axis=0
        )
        total = jnp.dot(lhs, w3[...], preferred_element_type=F32)
        for r in range(ROWS):
            direct[base + r] = total[r * 64 : r * 64 + 64, 0:128] * 0.5 + b3[...]
            turned[pl.ds(r, 64, stride=ROWS), :] = total[r * 64 : r * 64 + 64, 128:256] * 0.5
        for path in range(2):
            v = turned[path * 512 : path * 512 + 512, :]
            bufs[7 + path, t] = v.reshape(32, ROWS, 128).astype(BF16)

    def hop(n, t):
        code = out_codes[n]
        final = (code // 64) % 2
        which = (code // 128) % 4
        c = jnp.where(final == 1, t // 4, core)
        slot = jnp.where(final == 1, core * 2 + which, 4 + which)
        return pltpu.make_async_remote_copy(
            bufs.at[7 + n if n < 2 else 2 + n, t],
            bufs.at[slot, t],
            send_sem.at[n, t],
            recv_sem.at[slot, t],
            device_id=chip(code, c),
            device_id_type=MESH,
        )

    def across(n, t):
        return pltpu.make_async_remote_copy(
            bufs.at[7 + n, t],
            bufs.at[core * 2 + n, t],
            send_sem.at[n, t],
            recv_sem.at[core * 2 + n, t],
            device_id=(i, j + 1 - 2 * core),
            device_id_type=MESH,
        )

    def arrived(slot, t):
        pltpu.make_async_copy(bufs.at[slot, t], bufs.at[slot, t], recv_sem.at[slot, t]).wait()

    def send(t):
        for n in range(2):
            pl.when(jnp.logical_not(fixed))(lambda n=n: hop(n, t).start())
            pl.when(both(fixed, t // 4 != core))(lambda n=n: across(n, t).start())

            @pl.when(both(fixed, t // 4 == core))
            def _():
                pltpu.make_async_copy(
                    bufs.at[7 + n, t], bufs.at[core * 2 + n, t], recv_sem.at[core * 2 + n, t]
                ).start()

    def relay(s, t):
        @pl.when(out_codes[2 + s] >= 512)
        def _():
            arrived(4 + s, t)
            hop(2 + s, t).start()

    halo_wait([0, 1, 4, 5, 6])
    for row in range(1, 15):
        spread(row)
    near(2, 12)

    @pl.when(i == 0)
    def _():
        l1[2:8] = jnp.zeros((6, 80, 384), BF16)

    middle(4, 8)

    @pl.when(i == 0)
    def _():
        l2[4:8] = jnp.zeros((4, 64, 384), BF16)

    def step(t, carry):
        @pl.when(t == 1)
        def _():
            halo_wait([2, 3])

        @pl.when(t == 7)
        def _():
            halo_wait([7, 8, 9])

        base = t * ROWS
        for r in range(ROWS):
            spread(base + 15 + r)
        near(base + 14, ROWS)

        @pl.when(both(i == 7, t == 7))
        def _():
            l1[136:142] = jnp.zeros((6, 80, 384), BF16)

        middle(base + 12, ROWS)

        @pl.when(both(i == 7, t == 7))
        def _():
            l2[136:140] = jnp.zeros((4, 64, 384), BF16)

        far(t)
        send(t)
        for s in range(SLOTS):
            pl.when(t >= LAG[s])(lambda s=s: relay(s, t - LAG[s]))
        return carry

    lax.fori_loop(0, STEPS, step, 0)

    stores = []
    for late in range(6):
        for s in range(SLOTS):
            if late < LAG[s]:
                relay(s, STEPS + late - LAG[s])
        m = late - 2
        if m >= 0:
            t = core * 4 + m
            cols = slice(m * ROWS, m * ROWS + ROWS)
            for q in range(2):
                for path in range(2):
                    slot = q * 2 + path
                    arrived(slot, t)
                    rows = slice(slot * 32, slot * 32 + 32)
                    total = direct[rows, cols] + bufs[slot, t].astype(F32)
                    result[rows, cols] = total.astype(BF16)
            store = pltpu.make_async_copy(result.at[:, cols], out.at[:, cols], out_sem.at[m])
            store.start()
            stores.append(store)

    for copy, goes, _ in halo:
        pl.when(goes)(copy.wait_send)
    for t in range(STEPS):
        for n in range(2 + SLOTS):
            pl.when(out_codes[n] >= 512)(lambda n=n: hop(n, t).wait_send())
        for n in range(2):
            pl.when(both(fixed, t // 4 != core))(lambda n=n: across(n, t).wait_send())
    for store in stores:
        store.wait()


def local(contact_map, kernel_near, offset_near, kernel_mid, offset_mid, kernel_far, offset_far):
    anywhere, vmem = pl.BlockSpec(memory_space=pl.ANY), pl.BlockSpec(memory_space=pltpu.VMEM)
    args = [contact_map]
    for k, b in ((kernel_near, offset_near), (kernel_mid, offset_mid), (kernel_far, offset_far)):
        args += [k.reshape(9 * 128, 128), b.reshape(1, 128)]
    dma = pltpu.SemaphoreType.DMA
    return pl.pallas_call(
        kernel,
        out_shape=jax.ShapeDtypeStruct((128, 64, 128), BF16),
        in_specs=[anywhere] + [anywhere, vmem] * 3,
        out_specs=anywhere,
        scratch_shapes=[
            pltpu.VMEM((144, 64, 128), BF16),
            pltpu.VMEM((144, 8, 128), BF16),
            pltpu.VMEM((144, 8, 128), BF16),
            pltpu.VMEM((144, 80, 384), BF16),
            pltpu.VMEM((144, 80, 384), BF16),
            pltpu.VMEM((144, 64, 384), BF16),
            pltpu.VMEM((128, 64, 128), F32),
            pltpu.VMEM((1024, 128), F32),
            pltpu.VMEM((80, 128), F32),
            pltpu.VMEM((1536, 256), BF16),
            pltpu.VMEM((1536, 256), BF16),
            pltpu.VMEM((1152, 256), BF16),
            pltpu.VMEM((9, STEPS, 32, ROWS, 128), BF16),
            pltpu.VMEM((128, 64, 128), BF16),
            dma((15,)),
            dma((len(HALO),)),
            dma((len(HALO),)),
            dma((2 + SLOTS, STEPS)),
            dma((7, STEPS)),
            dma((4,)),
        ],
        compiler_params=pltpu.CompilerParams(
            collective_id=0, has_side_effects=True, vmem_limit_bytes=60 * 1024 * 1024
        ),
        name="trunk",
    )(*args)


def solution(mesh):
    in_specs = (P("row", "col", None), P(), P(), P(), P(), P(), P())
    return jax.shard_map(local, mesh=mesh, in_specs=in_specs, out_specs=P("row", "col", None), check_vma=False)
```

profile of v0, /device:TPU:7, one launch (start us, length us, event | category | flops | bytes accessed | tf_op | source)
XLA Modules:
  0.0 68.2 jit_solution(11986215990319065361)
XLA Ops:
  0.0 65.1 %trunk.1 = bf16[128,64,128]{2,1,0:T(8,128)(2,1)} custom-call(bf16[128,64,128]{2,1,0:T(8,128)(2,1)} %x.1, bf16[1152,128]{1,0:T(8,128)(2,1)} %bitcast.6, f32[1,128]{1,0:T(1,128)} %bitcast.9, bf16[1152,128]{1,0:T(8,128)(2,1)} %bitcast.7, f32[1,128]{1,0:T(1,128)} %bitcast.10, bf16[1152,128]{1,0:T(8,128)(2,1)} %bitcast.8, f32[1,128]{1,0:T(1,128)} %bitcast.11), custom_call_target="tpu_custom_call" | custom-call | tf_op jit(solution)/shard_map/trunk/pallas_call | solution.py:389
  65.1 3.1 %copy.9 = bf16[128,64,128]{2,1,0:T(8,128)(2,1)} copy(bf16[128,64,128]{2,1,0:T(8,128)(2,1)} %trunk.1) | data formatting | bytes 4194304
where the time goes:
time: 68.4 us; the launch traced here: 68.2 us
  Pallas kernels  65.1 us (95%)
  local copies, waits for them, and re-layouts  3.08 us (5%)
    pallas_call x1, Pallas kernels, local(): pl.pallas_call(kernel, out_shape=jax.ShapeDtypeStruct((128, 64, 128), BF1...  65.1 us
    unnamed x1, local copies, waits for them, and re-layouts  3.08 us

commit v1 on v0

--- a/solution.py
+++ b/solution.py
@@ -25,10 +25,11 @@
     6: ("y1 y0z0 x1", "z0 x1y0y1"),
     7: ("x1y1z1", "y1z1 x1"),
 }
-STEPS = 8
-ROWS = 16
-LAG = (2, 2, 4)
+STEPS = 16
+ROWS = 8
+LAG = (3, 3, 6)
 SLOTS = len(LAG)
+HALF = STEPS // 2
 
 
 def segment(text):
@@ -97,7 +98,7 @@
 
 ALL, LEFT, RIGHT = slice(0, 64), slice(0, 8), slice(56, 64)
 HALO = []
-for lo, hi in ((0, 32), (32, 128)):
+for lo, hi in ((0, 24), (24, 64), (64, 128)):
     HALO.append((0, -1, slice(lo, hi), LEFT, "r", slice(8 + lo, 8 + hi)))
     HALO.append((0, 1, slice(lo, hi), RIGHT, "l", slice(8 + lo, 8 + hi)))
 for di, src, dst in ((1, slice(120, 128), slice(0, 8)), (-1, slice(0, 8), slice(136, 144))):
@@ -107,9 +108,9 @@
 
 
 def kernel(
-    x, k1, b1, k2, b2, k3, b3, out,
-    xc, xl, xr, x3, l1, l2, direct, turned, inside, w1, w2, w3, bufs, result,
-    load_sem, halo_send, halo_recv, send_sem, recv_sem, out_sem,
+    x, k1, c1, k2, c2, k3, c3, out,
+    xc, xl, xr, x3, l1, l2, direct, turned, inside, w1, w2, w3, b1, b2, b3, bufs,
+    load_sem, halo_send, halo_recv, send_sem, recv_sem,
 ):
     i, j = lax.axis_index("row"), lax.axis_index("col")
     cx, cy, cz, core = i // 2, (j // 2) % 4, (i % 2) * 2 + j // 8, j % 2
@@ -125,7 +126,7 @@
         z_ = flipped(cz, (flips // 16) % 4)
         return (x_ * 2 + z_ // 2, (z_ % 2) * 8 + y_ * 2 + c)
 
-    loads = [(x, xc.at[8:136])]
+    loads = [(x, xc.at[8:136]), (c1, b1), (c2, b2), (c3, b3)]
     for k, wide in ((k1, w1), (k2, w2)):
         loads.append((k, wide.at[0:1152, 0:128]))
         loads.append((k, wide.at[384:1536, 128:256]))
@@ -203,7 +204,13 @@
         wide[1152:1536, 0:128] = jnp.zeros((384, 128), BF16)
         wide[0:384, 128:256] = jnp.zeros((384, 128), BF16)
     column = lax.broadcasted_iota(jnp.int32, (80, 128), 0) + (j * 64 - 8)
-    inside[...] = jnp.where(both(column >= 0, column < 1024), 1.0, 0.0).astype(F32)
+    inside[0] = jnp.zeros((80, 128), F32)
+    inside[1] = jnp.where(both(column >= 0, column < 1024), 1.0, 0.0).astype(F32)
+
+    def keep(row):
+        at = i * 128 + row - 8
+        return inside[jnp.where(both(at >= 0, at < 1024), 1, 0)]
+
     for copy in loads:
         copy.wait()
 
@@ -223,12 +230,11 @@
             [jnp.concatenate([ref[r + (n - 1) * d] for n in range(4)], axis=-1) for r in rows], axis=0
         )
         total = jnp.dot(lhs, wide[...], preferred_element_type=F32)
-        keep = inside[...]
         done = []
         for n, r in enumerate(rows):
             for m in range(2):
                 v = total[n * 80 : n * 80 + 80, m * 128 : m * 128 + 128]
-                done.append((r + m * d, jnp.maximum(v + bias[...], 0.0) * keep))
+                done.append((r + m * d, jnp.maximum(v + bias[...], 0.0) * keep(r + m * d)))
         return done
 
     def near(base, count):
@@ -254,21 +260,25 @@
             direct[base + r] = total[r * 64 : r * 64 + 64, 0:128] * 0.5 + b3[...]
             turned[pl.ds(r, 64, stride=ROWS), :] = total[r * 64 : r * 64 + 64, 128:256] * 0.5
         for path in range(2):
-            v = turned[path * 512 : path * 512 + 512, :]
+            v = turned[path * 32 * ROWS : (path + 1) * 32 * ROWS, :]
             bufs[7 + path, t] = v.reshape(32, ROWS, 128).astype(BF16)
 
+    goes_on = [code >= 512 for code in out_codes]
+    ends = [(code // 64) % 2 == 1 for code in out_codes]
+    where = [chip(code, 0) for code in out_codes]
+    slots = [
+        jnp.where(end, core * 2 + (code // 128) % 4, 4 + (code // 128) % 4) for code, end in zip(out_codes, ends)
+    ]
+
     def hop(n, t):
-        code = out_codes[n]
-        final = (code // 64) % 2
-        which = (code // 128) % 4
-        c = jnp.where(final == 1, t // 4, core)
-        slot = jnp.where(final == 1, core * 2 + which, 4 + which)
+        c = jnp.where(ends[n], t // HALF, core)
+        row, col = where[n]
         return pltpu.make_async_remote_copy(
             bufs.at[7 + n if n < 2 else 2 + n, t],
-            bufs.at[slot, t],
-            send_sem.at[n, t],
-            recv_sem.at[slot, t],
-            device_id=chip(code, c),
+            bufs.at[slots[n], t],
+            send_sem.at[n],
+            recv_sem.at[slots[n], t],
+            device_id=(row, col + c),
             device_id_type=MESH,
         )
 
@@ -276,121 +286,127 @@
         return pltpu.make_async_remote_copy(
             bufs.at[7 + n, t],
             bufs.at[core * 2 + n, t],
-            send_sem.at[n, t],
+            send_sem.at[n],
             recv_sem.at[core * 2 + n, t],
             device_id=(i, j + 1 - 2 * core),
             device_id_type=MESH,
         )
 
     def arrived(slot, t):
-        pltpu.make_async_copy(bufs.at[slot, t], bufs.at[slot, t], recv_sem.at[slot, t]).wait()
+        here = bufs.at[slot, t]
+        pltpu.make_async_copy(here, here, recv_sem.at[slot, t]).wait()
 
     def send(t):
-        for n in range(2):
-            pl.when(jnp.logical_not(fixed))(lambda n=n: hop(n, t).start())
-            pl.when(both(fixed, t // 4 != core))(lambda n=n: across(n, t).start())
-
-            @pl.when(both(fixed, t // 4 == core))
-            def _():
-                pltpu.make_async_copy(
-                    bufs.at[7 + n, t], bufs.at[core * 2 + n, t], recv_sem.at[core * 2 + n, t]
-                ).start()
-
-    def relay(s, t):
-        @pl.when(out_codes[2 + s] >= 512)
-        def _():
+        @pl.when(jnp.logical_not(fixed))
+        def _():
+            for n in range(2):
+                hop(n, t).start()
+
+        @pl.when(both(fixed, t // HALF != core))
+        def _():
+            for n in range(2):
+                across(n, t).start()
+
+        @pl.when(both(fixed, t // HALF == core))
+        def _():
+            for n in range(2):
+                own = core * 2 + n
+                pltpu.make_async_copy(bufs.at[7 + n, t], bufs.at[own, t], recv_sem.at[own, t]).start()
+
+    def relay(s, n):
+        @pl.when(both(goes_on[2 + s], both(n >= LAG[s], n < STEPS + LAG[s])))
+        def _():
+            t = lax.rem(n - LAG[s] + 1, STEPS)
             arrived(4 + s, t)
             hop(2 + s, t).start()
 
-    halo_wait([0, 1, 4, 5, 6])
-    for row in range(1, 15):
-        spread(row)
-    near(2, 12)
-
-    @pl.when(i == 0)
-    def _():
-        l1[2:8] = jnp.zeros((6, 80, 384), BF16)
-
-    middle(4, 8)
-
-    @pl.when(i == 0)
-    def _():
-        l2[4:8] = jnp.zeros((4, 64, 384), BF16)
-
-    def step(t, carry):
-        @pl.when(t == 1)
+    halo_wait([0, 1])
+
+    def step(n, carry):
+        @pl.when(n == 1)
         def _():
             halo_wait([2, 3])
 
-        @pl.when(t == 7)
-        def _():
-            halo_wait([7, 8, 9])
-
-        base = t * ROWS
+        @pl.when(n == 6)
+        def _():
+            halo_wait([4, 5])
+
+        @pl.when(n == 14)
+        def _():
+            halo_wait([9, 10, 11])
+
+        @pl.when(n == 15)
+        def _():
+            halo_wait([6, 7, 8])
+
+        last = n == STEPS - 1
+        base = (n + 1) * ROWS
         for r in range(ROWS):
-            spread(base + 15 + r)
-        near(base + 14, ROWS)
-
-        @pl.when(both(i == 7, t == 7))
-        def _():
-            l1[136:142] = jnp.zeros((6, 80, 384), BF16)
-
-        middle(base + 12, ROWS)
-
-        @pl.when(both(i == 7, t == 7))
-        def _():
-            l2[136:140] = jnp.zeros((4, 64, 384), BF16)
-
-        far(t)
-        send(t)
+            spread(jnp.where(last, 1, jnp.maximum(base + 15, 8)) + r)
+        near(jnp.where(last, 2, base + 14), ROWS)
+
+        @pl.when(n >= -1)
+        def _():
+            middle(jnp.where(last, 4, base + 12), ROWS)
+
+        @pl.when(n >= 0)
+        def _():
+            t = lax.rem(n + 1, STEPS)
+            far(t)
+            send(t)
+            for s in range(SLOTS):
+                relay(s, n)
+
+        return carry
+
+    lax.fori_loop(-2, STEPS, step, 0)
+
+    def drain(d, carry):
         for s in range(SLOTS):
-            pl.when(t >= LAG[s])(lambda s=s: relay(s, t - LAG[s]))
+            relay(s, STEPS + d)
+
+        @pl.when(d >= 1)
+        def _():
+            m = jnp.where(core == 0, lax.rem(d, HALF), d - 1)
+            t = core * HALF + m
+            cols = pl.ds(pl.multiple_of(m * ROWS, ROWS), ROWS)
+            for slot in range(4):
+                arrived(slot, t)
+                rows = slice(slot * 32, slot * 32 + 32)
+                out[rows, cols] = (direct[rows, cols] + bufs[slot, t].astype(F32)).astype(BF16)
+
         return carry
 
-    lax.fori_loop(0, STEPS, step, 0)
-
-    stores = []
-    for late in range(6):
-        for s in range(SLOTS):
-            if late < LAG[s]:
-                relay(s, STEPS + late - LAG[s])
-        m = late - 2
-        if m >= 0:
-            t = core * 4 + m
-            cols = slice(m * ROWS, m * ROWS + ROWS)
-            for q in range(2):
-                for path in range(2):
-                    slot = q * 2 + path
-                    arrived(slot, t)
-                    rows = slice(slot * 32, slot * 32 + 32)
-                    total = direct[rows, cols] + bufs[slot, t].astype(F32)
-                    result[rows, cols] = total.astype(BF16)
-            store = pltpu.make_async_copy(result.at[:, cols], out.at[:, cols], out_sem.at[m])
-            store.start()
-            stores.append(store)
+    lax.fori_loop(0, HALF + 1, drain, 0)
 
     for copy, goes, _ in halo:
         pl.when(goes)(copy.wait_send)
-    for t in range(STEPS):
-        for n in range(2 + SLOTS):
-            pl.when(out_codes[n] >= 512)(lambda n=n: hop(n, t).wait_send())
+    for n in range(2 + SLOTS):
+
+        @pl.when(goes_on[n])
+        def _():
+            sent = bufs.at[7 + n if n < 2 else 2 + n]
+            pltpu.make_async_copy(sent, sent, send_sem.at[n]).wait()
+
+    @pl.when(fixed)
+    def _():
         for n in range(2):
-            pl.when(both(fixed, t // 4 != core))(lambda n=n: across(n, t).wait_send())
-    for store in stores:
-        store.wait()
+            sent = bufs.at[7 + n, 0:HALF]
+            pltpu.make_async_copy(sent, sent, send_sem.at[n]).wait()
 
 
 def local(contact_map, kernel_near, offset_near, kernel_mid, offset_mid, kernel_far, offset_far):
-    anywhere, vmem = pl.BlockSpec(memory_space=pl.ANY), pl.BlockSpec(memory_space=pltpu.VMEM)
+    hbm, vmem = pl.BlockSpec(memory_space=pltpu.HBM), pl.BlockSpec(memory_space=pltpu.VMEM)
     args = [contact_map]
     for k, b in ((kernel_near, offset_near), (kernel_mid, offset_mid), (kernel_far, offset_far)):
         args += [k.reshape(9 * 128, 128), b.reshape(1, 128)]
+    args = [pltpu.with_memory_space_constraint(v, pltpu.HBM) for v in args]
     dma = pltpu.SemaphoreType.DMA
     return pl.pallas_call(
         kernel,
         out_shape=jax.ShapeDtypeStruct((128, 64, 128), BF16),
-        in_specs=[anywhere] + [anywhere, vmem] * 3,
-        out_specs=anywhere,
+        in_specs=[hbm] * 7,
+        out_specs=vmem,
         scratch_shapes=[
             pltpu.VMEM((144, 64, 128), BF16),
             pltpu.VMEM((144, 8, 128), BF16),
@@ -399,22 +415,23 @@
             pltpu.VMEM((144, 80, 384), BF16),
             pltpu.VMEM((144, 64, 384), BF16),
             pltpu.VMEM((128, 64, 128), F32),
-            pltpu.VMEM((1024, 128), F32),
-            pltpu.VMEM((80, 128), F32),
+            pltpu.VMEM((64 * ROWS, 128), F32),
+            pltpu.VMEM((2, 80, 128), F32),
             pltpu.VMEM((1536, 256), BF16),
             pltpu.VMEM((1536, 256), BF16),
             pltpu.VMEM((1152, 256), BF16),
+            pltpu.VMEM((1, 128), F32),
+            pltpu.VMEM((1, 128), F32),
+            pltpu.VMEM((1, 128), F32),
             pltpu.VMEM((9, STEPS, 32, ROWS, 128), BF16),
-            pltpu.VMEM((128, 64, 128), BF16),
-            dma((15,)),
+            dma((18,)),
             dma((len(HALO),)),
             dma((len(HALO),)),
-            dma((2 + SLOTS, STEPS)),
+            dma((2 + SLOTS,)),
             dma((7, STEPS)),
-            dma((4,)),
         ],
         compiler_params=pltpu.CompilerParams(
-            collective_id=0, has_side_effects=True, vmem_limit_bytes=60 * 1024 * 1024
+            collective_id=0, has_side_effects=True, vmem_limit_bytes=50 * 1024 * 1024
         ),
         name="trunk",
     )(*args)

time: 68.4 us -> 52.5 us (0.77)
  the two profiles are of different devices: /device:TPU:7 before, /device:TPU:48 now
where the time goes in v1:
time: 52.5 us; the launch traced here: 52.4 us
  Pallas kernels  51 us (97%)
  local copies, waits for them, and re-layouts  1.32 us (3%)
    pallas_call x1, Pallas kernels, local(): pl.pallas_call(kernel, out_shape=jax.ShapeDtypeStruct((128, 64, 128), BF1...  51 us
    unnamed x1, local copies, waits for them, and re-layouts  1.32 us

profile of v1, /device:TPU:48, one launch (start us, length us, event | category | flops | bytes accessed | tf_op | source)
XLA Modules:
  0.0 52.4 jit_solution(1613425940764733339)
XLA Ops:
  0.0 51.0 %trunk.1 = bf16[128,64,128]{2,1,0:T(8,128)(2,1)S(1)} custom-call(bf16[128,64,128]{2,1,0:T(8,128)(2,1)} %x.1, bf16[1152,128]{1,0:T(8,128)(2,1)} %bitcast.6, f32[1,128]{1,0:T(1,128)} %bitcast.9, bf16[1152,128]{1,0:T(8,128)(2,1)} %bitcast.7, f32[1,128]{1,0:T(1,128)} %bitcast.10, bf16[1152,128]{1,0:T(8,128)(2,1)} %bitcast.8, f32[1,128]{1,0:T(1,128)} %bitcast.11), custom_call_target="tpu_custom_call" | custom-call | tf_op jit(solution)/shard_map/trunk/pallas_call | solution.py:405
  51.1 1.3 %copy.9 = bf16[128,64,128]{2,1,0:T(8,128)(2,1)} copy(bf16[128,64,128]{2,1,0:T(8,128)(2,1)S(1)} %trunk.1) | data formatting | bytes 4194304

commit v2 on v1

--- a/solution.py
+++ b/solution.py
@@ -28,6 +28,8 @@
 STEPS = 16
 ROWS = 8
 LAG = (3, 3, 6)
+AHEAD = 3
+DIRECT = 2
 SLOTS = len(LAG)
 HALF = STEPS // 2
 
@@ -79,6 +81,11 @@
 
 
 OUT, INTO = plan()
+STRAIGHT = [0] * 8
+for start, paths in PATHS.items():
+    if len(paths[0].split()) == 3:
+        flips, _ = segment(paths[0].replace(" ", ""))
+        STRAIGHT[start] = flips[0] + 4 * flips[1] + 16 * flips[2] + 64
 
 
 def pick(w, values):
@@ -110,7 +117,7 @@
 def kernel(
     x, k1, c1, k2, c2, k3, c3, out,
     xc, xl, xr, x3, l1, l2, direct, turned, inside, w1, w2, w3, b1, b2, b3, bufs,
-    load_sem, halo_send, halo_recv, send_sem, recv_sem,
+    load_sem, halo_send, halo_recv, send_sem, side_sem, recv_sem,
 ):
     i, j = lax.axis_index("row"), lax.axis_index("col")
     cx, cy, cz, core = i // 2, (j // 2) % 4, (i % 2) * 2 + j // 8, j % 2
@@ -165,7 +172,15 @@
     def _():
         greet((i, j + 1 - 2 * core))
 
-    expected = expected + jnp.where(fixed, 1, 0)
+    straight = pick(w, STRAIGHT)
+    long = straight >= 64
+
+    @pl.when(long)
+    def _():
+        greet(chip(straight, 0))
+        greet(chip(straight, 1))
+
+    expected = expected + jnp.where(fixed, 1, 0) + jnp.where(long, 2, 0)
     for n in range(2 + SLOTS):
         came, goes = in_codes[n], out_codes[n]
 
@@ -270,15 +285,20 @@
         jnp.where(end, core * 2 + (code // 128) % 4, 4 + (code // 128) % 4) for code, end in zip(out_codes, ends)
     ]
 
-    def hop(n, t):
-        c = jnp.where(ends[n], t // HALF, core)
+    target = chip(straight, 0)
+
+    def hop(n, t, direct=None):
         row, col = where[n]
+        end, slot = ends[n], slots[n]
+        if direct is not None:
+            row, col = jnp.where(direct, target[0], row), jnp.where(direct, target[1], col)
+            end, slot = jnp.logical_or(direct, end), jnp.where(direct, core * 2, slot)
         return pltpu.make_async_remote_copy(
             bufs.at[7 + n if n < 2 else 2 + n, t],
-            bufs.at[slots[n], t],
-            send_sem.at[n],
-            recv_sem.at[slots[n], t],
-            device_id=(row, col + c),
+            bufs.at[slot, t],
+            send_sem.at[n, t],
+            recv_sem.at[slot, t],
+            device_id=(row, col + jnp.where(end, t // HALF, core)),
             device_id_type=MESH,
         )
 
@@ -286,7 +306,7 @@
         return pltpu.make_async_remote_copy(
             bufs.at[7 + n, t],
             bufs.at[core * 2 + n, t],
-            send_sem.at[n],
+            side_sem.at[n],
             recv_sem.at[core * 2 + n, t],
             device_id=(i, j + 1 - 2 * core),
             device_id_type=MESH,
@@ -296,11 +316,21 @@
         here = bufs.at[slot, t]
         pltpu.make_async_copy(here, here, recv_sem.at[slot, t]).wait()
 
-    def send(t):
+    def left(op, n):
+        hop(op, lax.rem(n + 1, STEPS)).wait_send()
+
+    def send(n):
+        t = lax.rem(n + 1, STEPS)
+
+        @pl.when(both(jnp.logical_not(fixed), n >= AHEAD))
+        def _():
+            for op in range(2):
+                left(op, n - AHEAD)
+
         @pl.when(jnp.logical_not(fixed))
         def _():
-            for n in range(2):
-                hop(n, t).start()
+            hop(0, t, both(long, n >= STEPS - DIRECT)).start()
+            hop(1, t).start()
 
         @pl.when(both(fixed, t // HALF != core))
         def _():
@@ -313,53 +343,62 @@
                 own = core * 2 + n
                 pltpu.make_async_copy(bufs.at[7 + n, t], bufs.at[own, t], recv_sem.at[own, t]).start()
 
+    steps = [
+        jnp.int32(STEPS - DIRECT) if s == 2 else jnp.where(ends[2 + s], STEPS, STEPS - DIRECT) for s in range(SLOTS)
+    ]
+
     def relay(s, n):
-        @pl.when(both(goes_on[2 + s], both(n >= LAG[s], n < STEPS + LAG[s])))
+        @pl.when(both(goes_on[2 + s], both(n >= LAG[s], n < steps[s] + LAG[s])))
         def _():
             t = lax.rem(n - LAG[s] + 1, STEPS)
             arrived(4 + s, t)
+            pl.when(n >= LAG[s] + AHEAD)(lambda: left(2 + s, n - LAG[s] - AHEAD))
             hop(2 + s, t).start()
 
+    def first(n, low, offset):
+        return jnp.where(n >= STEPS - 1, low, (n + 1) * ROWS + offset)
+
+    def feed(n):
+        base = jnp.maximum(first(n, 1, 15), jnp.where(n < 0, 8, 0))
+        for r in range(ROWS):
+            spread(base + r)
+
+    def one(n):
+        near(first(n, 2, 14), ROWS)
+
+    def two(n):
+        middle(first(n, 4, 12), ROWS)
+
     halo_wait([0, 1])
+    feed(jnp.int32(-2))
+
+    def fill(n, carry):
+        @pl.when(n == 0)
+        def _():
+            halo_wait([2, 3])
+
+        one(n)
+        feed(n + 1)
+        pl.when(n >= -1)(lambda: two(n))
+        return carry
+
+    lax.fori_loop(-2, 1, fill, 0)
 
     def step(n, carry):
-        @pl.when(n == 1)
-        def _():
-            halo_wait([2, 3])
-
-        @pl.when(n == 6)
-        def _():
-            halo_wait([4, 5])
-
-        @pl.when(n == 14)
-        def _():
-            halo_wait([9, 10, 11])
-
-        @pl.when(n == 15)
-        def _():
-            halo_wait([6, 7, 8])
-
-        last = n == STEPS - 1
-        base = (n + 1) * ROWS
-        for r in range(ROWS):
-            spread(jnp.where(last, 1, jnp.maximum(base + 15, 8)) + r)
-        near(jnp.where(last, 2, base + 14), ROWS)
-
-        @pl.when(n >= -1)
-        def _():
-            middle(jnp.where(last, 4, base + 12), ROWS)
-
-        @pl.when(n >= 0)
-        def _():
-            t = lax.rem(n + 1, STEPS)
-            far(t)
-            send(t)
-            for s in range(SLOTS):
-                relay(s, n)
-
+        for at, which in ((4, [4, 5]), (12, [9, 10, 11]), (13, [6, 7, 8])):
+            pl.when(n == at)(lambda which=which: halo_wait(which))
+        t = lax.rem(n + 1, STEPS)
+        far(t)
+        one(n + 1)
+        feed(n + 2)
+        send(n)
+        relay(2, n)
+        pl.when(n >= 0)(lambda: two(n + 1))
+        relay(0, n)
+        relay(1, n)
         return carry
 
-    lax.fori_loop(-2, STEPS, step, 0)
+    lax.fori_loop(0, STEPS, step, 0)
 
     def drain(d, carry):
         for s in range(SLOTS):
@@ -381,18 +420,18 @@
 
     for copy, goes, _ in halo:
         pl.when(goes)(copy.wait_send)
-    for n in range(2 + SLOTS):
-
-        @pl.when(goes_on[n])
-        def _():
-            sent = bufs.at[7 + n if n < 2 else 2 + n]
-            pltpu.make_async_copy(sent, sent, send_sem.at[n]).wait()
+    for op in range(2 + SLOTS):
+
+        @pl.when(goes_on[op])
+        def _():
+            for n in range(AHEAD):
+                left(op, (STEPS if op < 2 else steps[op - 2]) - AHEAD + n)
 
     @pl.when(fixed)
     def _():
         for n in range(2):
             sent = bufs.at[7 + n, 0:HALF]
-            pltpu.make_async_copy(sent, sent, send_sem.at[n]).wait()
+            pltpu.make_async_copy(sent, sent, side_sem.at[n]).wait()
 
 
 def local(contact_map, kernel_near, offset_near, kernel_mid, offset_mid, kernel_far, offset_far):
@@ -427,7 +466,8 @@
             dma((18,)),
             dma((len(HALO),)),
             dma((len(HALO),)),
-            dma((2 + SLOTS,)),
+            dma((2 + SLOTS, STEPS)),
+            dma((2,)),
             dma((7, STEPS)),
         ],
         compiler_params=pltpu.CompilerParams(

time: 52.5 us -> 50.3 us (0.958)
  the two profiles are of different devices: /device:TPU:48 before, /device:TPU:26 now
where the time goes in v2:
time: 50.3 us; the launch traced here: 50.2 us
  Pallas kernels  48.9 us (97%)
  local copies, waits for them, and re-layouts  1.32 us (3%)
    pallas_call x1, Pallas kernels, local(): pl.pallas_call(kernel, out_shape=jax.ShapeDtypeStruct((128, 64, 128), BF1...  48.9 us
    unnamed x1, local copies, waits for them, and re-layouts  1.32 us

profile of v2, /device:TPU:26, one launch (start us, length us, event | category | flops | bytes accessed | tf_op | source)
XLA Modules:
  0.0 50.2 jit_solution(947331286904488657)
XLA Ops:
  0.0 48.9 %trunk.1 = bf16[128,64,128]{2,1,0:T(8,128)(2,1)S(1)} custom-call(bf16[128,64,128]{2,1,0:T(8,128)(2,1)} %x.1, bf16[1152,128]{1,0:T(8,128)(2,1)} %bitcast.6, f32[1,128]{1,0:T(1,128)} %bitcast.9, bf16[1152,128]{1,0:T(8,128)(2,1)} %bitcast.7, f32[1,128]{1,0:T(1,128)} %bitcast.10, bf16[1152,128]{1,0:T(8,128)(2,1)} %bitcast.8, f32[1,128]{1,0:T(1,128)} %bitcast.11), custom_call_target="tpu_custom_call" | custom-call | tf_op jit(solution)/shard_map/trunk/pallas_call | solution.py:444
  48.9 1.3 %copy.9 = bf16[128,64,128]{2,1,0:T(8,128)(2,1)} copy(bf16[128,64,128]{2,1,0:T(8,128)(2,1)S(1)} %trunk.1) | data formatting | bytes 4194304

commit v3 on v2

--- a/solution.py
+++ b/solution.py
@@ -393,7 +393,7 @@
         feed(n + 2)
         send(n)
         relay(2, n)
-        pl.when(n >= 0)(lambda: two(n + 1))
+        pl.when(n < STEPS - 1)(lambda: two(n + 1))
         relay(0, n)
         relay(1, n)
         return carry
@@ -454,7 +454,7 @@
             pltpu.VMEM((144, 80, 384), BF16),
             pltpu.VMEM((144, 64, 384), BF16),
             pltpu.VMEM((128, 64, 128), F32),
-            pltpu.VMEM((64 * ROWS, 128), F32),
+            pltpu.VMEM((65 * ROWS, 128), F32),
             pltpu.VMEM((2, 80, 128), F32),
             pltpu.VMEM((1536, 256), BF16),
             pltpu.VMEM((1536, 256), BF16),

time: 50.3 us -> 50.4 us (level)
  no operation moved by 1% of the time
where the time goes in v3:
time: 50.4 us; the launch traced here: 50.3 us
  Pallas kernels  48.9 us (97%)
  local copies, waits for them, and re-layouts  1.32 us (3%)
    pallas_call x1, Pallas kernels, local(): pl.pallas_call(kernel, out_shape=jax.ShapeDtypeStruct((128, 64, 128), BF1...  48.9 us
    unnamed x1, local copies, waits for them, and re-layouts  1.32 us

profile of v3, /device:TPU:26, one launch (start us, length us, event | category | flops | bytes accessed | tf_op | source)
XLA Modules:
  0.0 50.3 jit_solution(4930180394847045696)
XLA Ops:
  0.0 48.9 %trunk.1 = bf16[128,64,128]{2,1,0:T(8,128)(2,1)S(1)} custom-call(bf16[128,64,128]{2,1,0:T(8,128)(2,1)} %x.1, bf16[1152,128]{1,0:T(8,128)(2,1)} %bitcast.6, f32[1,128]{1,0:T(1,128)} %bitcast.9, bf16[1152,128]{1,0:T(8,128)(2,1)} %bitcast.7, f32[1,128]{1,0:T(1,128)} %bitcast.10, bf16[1152,128]{1,0:T(8,128)(2,1)} %bitcast.8, f32[1,128]{1,0:T(1,128)} %bitcast.11), custom_call_target="tpu_custom_call" | custom-call | tf_op jit(solution)/shard_map/trunk/pallas_call | solution.py:444
  48.9 1.3 %copy.9 = bf16[128,64,128]{2,1,0:T(8,128)(2,1)} copy(bf16[128,64,128]{2,1,0:T(8,128)(2,1)S(1)} %trunk.1) | data formatting | bytes 4194304

commit v4 on v3

--- a/solution.py
+++ b/solution.py
@@ -27,9 +27,9 @@
 }
 STEPS = 16
 ROWS = 8
-LAG = (3, 3, 6)
+LAG = (3, 3, 5)
 AHEAD = 3
-DIRECT = 2
+DIRECT = 1
 SLOTS = len(LAG)
 HALF = STEPS // 2
 
@@ -105,10 +105,10 @@
 
 ALL, LEFT, RIGHT = slice(0, 64), slice(0, 8), slice(56, 64)
 HALO = []
-for lo, hi in ((0, 24), (24, 64), (64, 128)):
+for lo, hi in ((0, 24), (24, 48), (48, 128)):
     HALO.append((0, -1, slice(lo, hi), LEFT, "r", slice(8 + lo, 8 + hi)))
     HALO.append((0, 1, slice(lo, hi), RIGHT, "l", slice(8 + lo, 8 + hi)))
-for di, src, dst in ((1, slice(120, 128), slice(0, 8)), (-1, slice(0, 8), slice(136, 144))):
+for di, src, dst in ((1, slice(121, 128), slice(1, 8)), (-1, slice(0, 7), slice(136, 143))):
     HALO.append((di, 0, src, ALL, "c", dst))
     HALO.append((di, -1, src, LEFT, "r", dst))
     HALO.append((di, 1, src, RIGHT, "l", dst))
@@ -385,15 +385,15 @@
     lax.fori_loop(-2, 1, fill, 0)
 
     def step(n, carry):
-        for at, which in ((4, [4, 5]), (12, [9, 10, 11]), (13, [6, 7, 8])):
+        for at, which in ((2, [4, 5]), (12, [9, 10, 11]), (13, [6, 7, 8])):
             pl.when(n == at)(lambda which=which: halo_wait(which))
         t = lax.rem(n + 1, STEPS)
         far(t)
         one(n + 1)
         feed(n + 2)
         send(n)
+        pl.when(n < STEPS - 1)(lambda: two(n + 1))
         relay(2, n)
-        pl.when(n < STEPS - 1)(lambda: two(n + 1))
         relay(0, n)
         relay(1, n)
         return carry

time: 50.4 us -> 50.1 us (level); the launches traced: 50.3 us -> 49.1 us
  Pallas kernels: 48.9 us -> 47.7 us
    pallas_call x1, Pallas kernels: 48.9 us -> 47.7 us  [local(): pl.pallas_call(kernel, out_shape=jax.ShapeDtypeStruct((128, 64, 128), BF1...]
where the time goes in v4:
time: 50.1 us; the launch traced here: 49.1 us
  Pallas kernels  47.7 us (95%)
  local copies, waits for them, and re-layouts  1.32 us (3%)
    pallas_call x1, Pallas kernels, local(): pl.pallas_call(kernel, out_shape=jax.ShapeDtypeStruct((128, 64, 128), BF1...  47.7 us
    unnamed x1, local copies, waits for them, and re-layouts  1.32 us

profile of v4, /device:TPU:26, one launch (start us, length us, event | category | flops | bytes accessed | tf_op | source)
XLA Modules:
  0.0 49.1 jit_solution(14575653064247947649)
XLA Ops:
  0.0 47.7 %trunk.1 = bf16[128,64,128]{2,1,0:T(8,128)(2,1)S(1)} custom-call(bf16[128,64,128]{2,1,0:T(8,128)(2,1)} %x.1, bf16[1152,128]{1,0:T(8,128)(2,1)} %bitcast.6, f32[1,128]{1,0:T(1,128)} %bitcast.9, bf16[1152,128]{1,0:T(8,128)(2,1)} %bitcast.7, f32[1,128]{1,0:T(1,128)} %bitcast.10, bf16[1152,128]{1,0:T(8,128)(2,1)} %bitcast.8, f32[1,128]{1,0:T(1,128)} %bitcast.11), custom_call_target="tpu_custom_call" | custom-call | tf_op jit(solution)/shard_map/trunk/pallas_call | solution.py:444
  47.7 1.3 %copy.9 = bf16[128,64,128]{2,1,0:T(8,128)(2,1)} copy(bf16[128,64,128]{2,1,0:T(8,128)(2,1)S(1)} %trunk.1) | data formatting | bytes 4194304
